TPU v7x, 32 devices: a whole 2x2x4 slice. The times are simulated.
32 devices in a mesh: dom: 8 (over z, y), rows: 4 (over x, core).
Axes of the slice: x: 2, y: 2, z: 4, core: 2. Of those that a mesh axis runs over, the one named last changes fastest.
Arguments:
- fields: float32 [8, 3, 128, 4096], P('dom', None, 'rows'), may hold values from -6 to 6
- depth: float32 [128, 4096], P('rows'), may hold values from 1.5 to 6
- obs_index: int32 [256], replicated, may hold values from 0 to 524287, as said below
- obs_value: float32 [256], replicated, may hold values from -6 to 6
- obs_var: float32 [256], replicated, may hold values from 0.5 to 5
- parent_lookup: int32 [8], replicated, may hold values from 0 to 7, as said below
Outputs:
- log_weights: float32 [8], P('dom')
- posterior_members: float32 [8, 3, 128, 4096], P('dom', None, 'rows')
Inputs may be any that keep to these rules, and one draw needn't show every extreme that they name: `parent_lookup`: every value is the index of a particle; 0 and 7 each appear; values may repeat. `obs_index`: indices of grid cells, possibly repeated; the first and last cell each appear.
All inputs are finite; a program needn't handle non-finite values.
Results may differ from a plain program's by a relative error of at most 0.00003.
Values sent between devices are 32-bit elements; how exact they have to be, the bound alone decides.
No kernel may reach another device: no remote copies, remote signals or barrier semaphores. Data moves between devices by JAX's collectives and lax.ppermute only.
A program may use at most 64 MiB of HBM per device.

v0:
```python
import jax
import jax.numpy as jnp
from jax import lax
from jax.sharding import PartitionSpec as P

STEPS = 4
time_step = 0.5
coriolis = 0.2


def extended(cells, sides, width):
    for axis, dim in sides:
        count = lax.axis_size(axis)
        ends = count - 1
        head = lax.slice_in_dim(cells, 0, width, axis=dim)
        tail = lax.slice_in_dim(cells, cells.shape[dim] - width, cells.shape[dim], axis=dim)
        cells = jnp.concatenate(
            [
                lax.ppermute(tail, axis, [(i, (i + 1) % count) for i in range(ends)]),
                cells,
                lax.ppermute(head, axis, [((i + 1) % count, i) for i in range(ends)]),
            ],
            axis=dim,
        )
    return cells


def cols_diff(a):
    return 0.5 * (jnp.roll(a, -1, axis=-1) - jnp.roll(a, 1, axis=-1))


def flux_rows_diff(a):
    padded = extended(a, (("rows", 1),), 1)
    return 0.5 * (padded[:, 2:] - padded[:, :-2])


def height_rows_diff(a):
    padded = extended(a, (("rows", 1),), 1)
    return 0.5 * (padded[:, 2:] - padded[:, :-2])


def shards(fields, depth, obs_index, obs_value, obs_var, parent_lookup):
    free_elevation = fields[:, 0]
    zonal_current = fields[:, 1]
    meridional_current = fields[:, 2]
    depth_rows = depth[None]
    for step in range(STEPS):
        free_elevation = free_elevation - time_step * (
            cols_diff(depth_rows * zonal_current) + flux_rows_diff(depth_rows * meridional_current)
        )
        zonal_current = (
            zonal_current
            - time_step * cols_diff(free_elevation)
            + time_step * coriolis * meridional_current
        )
        meridional_current = (
            meridional_current
            - time_step * height_rows_diff(free_elevation)
            - time_step * coriolis * zonal_current
        )
    prior_members = jnp.stack([free_elevation, zonal_current, meridional_current], axis=1)
    slab_cells = free_elevation.shape[1] * free_elevation.shape[2]
    flat = free_elevation.reshape(free_elevation.shape[0], slab_cells)
    offset = obs_index - lax.axis_index("rows") * slab_cells
    inside = (offset >= 0) & (offset < slab_cells)
    values = jnp.take(flat, jnp.clip(offset, 0, slab_cells - 1), axis=1)
    misfit = jnp.where(inside[None, :], (obs_value[None, :] - values) ** 2 / obs_var[None, :], 0.0)
    loglik = lax.psum(-0.5 * jnp.sum(misfit, axis=1), "rows")
    local_peak = jnp.max(loglik)
    peak = lax.pmax(local_peak, "dom")
    total = lax.psum(jnp.sum(jnp.exp(loglik - peak)), "dom")
    log_weights = loglik - (peak + jnp.log(total))
    member_batches = lax.axis_size("dom")
    subregion_tiles = prior_members.reshape(prior_members.shape[0], member_batches, -1)
    received = lax.all_to_all(subregion_tiles, "dom", split_axis=1, concat_axis=0, tiled=True)
    picked = jnp.take(received, parent_lookup, axis=0)
    final_answer = lax.all_to_all(picked, "dom", split_axis=0, concat_axis=1, tiled=True)
    posterior_members = final_answer.reshape(prior_members.shape)
    return (log_weights, posterior_members)


def solution(mesh):
    in_specs = (P("dom", None, "rows", None), P("rows", None), P(), P(), P(), P())
    out_specs = (P("dom"), P("dom", None, "rows", None))
    return jax.shard_map(shards, mesh=mesh, in_specs=in_specs, out_specs=out_specs, check_vma=False)
```

profile of v0, /device:TPU:0, one launch (start us, length us, event | category | flops | bytes accessed | tf_op | source)
XLA Modules:
  0.0 196.9 jit_solution(10956344238698657955)
XLA Ops:
  0.6 1.5 fusion.51
  2.1 1.4 collective-permute-start
  3.6 3.0 %collective-permute-start.1 = (f32[1,1,4096]{2,1,0:T(1,128)S(1)}, f32[1,1,4096]{2,1,0:T(1,128)S(1)}, u32[]{:S(2)}, u32[]{:S(2)}) collective-permute-start(f32[1,1,4096]{2,1,0:T(1,128)S(1)} %get-tuple-element.68), channel_id=1, source_target_pairs={{0,1},{1,2},{2,3},{4,5},{5,6},{6,7},{8,9},{9,10},{10,11},{12,13},{... | collective-permute-start | bytes 49160 | tf_op jit(solution)/shard_map/ppermute | solution.py:19
  6.9 0.5 collective-permute-done.1
  7.4 0.2 fusion.32
  7.8 0.2 slice_bitcast_fusion.2
  8.0 1.3 collective-permute-start.2
  9.3 5.1 %collective-permute-start.3 = (f32[1,1,4096]{2,1,0:T(1,128)S(1)}, f32[1,1,4096]{2,1,0:T(1,128)S(1)}, u32[]{:S(2)}, u32[]{:S(2)}) collective-permute-start(f32[1,1,4096]{2,1,0:T(1,128)S(1)} %get-tuple-element.62), channel_id=1, source_target_pairs={{0,1},{1,2},{2,3},{4,5},{5,6},{6,7},{8,9},{9,10},{10,11},{12,13},{... | collective-permute-start | bytes 49160 | tf_op jit(solution)/shard_map/ppermute | solution.py:19
  14.9 0.4 collective-permute-done.3
  15.3 0.3 bitcast_multiply_fusion.5
  15.7 1.3 collective-permute-start.4
  17.0 4.9 %collective-permute-start.5 = (f32[1,1,4096]{2,1,0:T(1,128)S(1)}, f32[1,1,4096]{2,1,0:T(1,128)S(1)}, u32[]{:S(2)}, u32[]{:S(2)}) collective-permute-start(f32[1,1,4096]{2,1,0:T(1,128)S(1)} %get-tuple-element.60), channel_id=1, source_target_pairs={{0,1},{1,2},{2,3},{4,5},{5,6},{6,7},{8,9},{9,10},{10,11},{12,13},{... | collective-permute-start | bytes 49160 | tf_op jit(solution)/shard_map/ppermute | solution.py:19
  21.9 0.7 collective-permute-done.5
  22.6 0.2 fusion.24
  23.2 1.3 collective-permute-start.6
  24.5 4.9 %collective-permute-start.7 = (f32[1,1,4096]{2,1,0:T(1,128)S(1)}, f32[1,1,4096]{2,1,0:T(1,128)S(1)}, u32[]{:S(2)}, u32[]{:S(2)}) collective-permute-start(f32[1,1,4096]{2,1,0:T(1,128)S(1)} %get-tuple-element.42), channel_id=1, source_target_pairs={{0,1},{1,2},{2,3},{4,5},{5,6},{6,7},{8,9},{9,10},{10,11},{12,13},{... | collective-permute-start | bytes 49160 | tf_op jit(solution)/shard_map/ppermute | solution.py:19
  29.4 0.2 bitcast_multiply_fusion.4
  29.8 0.4 collective-permute-done.7
  30.4 1.3 collective-permute-start.8
  31.7 4.9 %collective-permute-start.9 = (f32[1,1,4096]{2,1,0:T(1,128)S(1)}, f32[1,1,4096]{2,1,0:T(1,128)S(1)}, u32[]{:S(2)}, u32[]{:S(2)}) collective-permute-start(f32[1,1,4096]{2,1,0:T(1,128)S(1)} %get-tuple-element.40), channel_id=1, source_target_pairs={{0,1},{1,2},{2,3},{4,5},{5,6},{6,7},{8,9},{9,10},{10,11},{12,13},{... | collective-permute-start | bytes 49160 | tf_op jit(solution)/shard_map/ppermute | solution.py:19
  36.7 0.7 collective-permute-done.9
  37.4 0.3 fusion.16
  38.0 1.3 collective-permute-start.10
  39.3 4.9 %collective-permute-start.11 = (f32[1,1,4096]{2,1,0:T(1,128)S(1)}, f32[1,1,4096]{2,1,0:T(1,128)S(1)}, u32[]{:S(2)}, u32[]{:S(2)}) collective-permute-start(f32[1,1,4096]{2,1,0:T(1,128)S(1)} %get-tuple-element.30), channel_id=1, source_target_pairs={{0,1},{1,2},{2,3},{4,5},{5,6},{6,7},{8,9},{9,10},{10,11},{12,13},{... | collective-permute-start | bytes 49160 | tf_op jit(solution)/shard_map/ppermute | solution.py:19
  44.6 0.4 collective-permute-done.11
  45.2 1.3 collective-permute-start.12
  46.5 4.9 %collective-permute-start.13 = (f32[1,1,4096]{2,1,0:T(1,128)S(1)}, f32[1,1,4096]{2,1,0:T(1,128)S(1)}, u32[]{:S(2)}, u32[]{:S(2)}) collective-permute-start(f32[1,1,4096]{2,1,0:T(1,128)S(1)} %get-tuple-element.28), channel_id=1, source_target_pairs={{0,1},{1,2},{2,3},{4,5},{5,6},{6,7},{8,9},{9,10},{10,11},{12,13},{... | collective-permute-start | bytes 49160 | tf_op jit(solution)/shard_map/ppermute | solution.py:19
  51.5 0.7 collective-permute-done.13
  52.2 0.3 fusion.8
  52.7 1.3 collective-permute-start.14
  54.0 4.9 %collective-permute-start.15 = (f32[1,1,4096]{2,1,0:T(1,128)S(1)}, f32[1,1,4096]{2,1,0:T(1,128)S(1)}, u32[]{:S(2)}, u32[]{:S(2)}) collective-permute-start(f32[1,1,4096]{2,1,0:T(1,128)S(1)} %get-tuple-element.22), channel_id=1, source_target_pairs={{0,1},{1,2},{2,3},{4,5},{5,6},{6,7},{8,9},{9,10},{10,11},{12,13},{... | collective-permute-start | bytes 49160 | tf_op jit(solution)/shard_map/ppermute | solution.py:19
  59.0 0.7 collective-permute-done.15
  59.7 0.3 fusion.4
  60.2 2.8 %reshape.582 = f32[1,8,49152]{2,0,1:T(1,128)} reshape(f32[1,3,32,4096]{3,2,1,0:T(8,128)S(1)} %pad_maximum_fusion) | data formatting | bytes 3145728 | tf_op jit(solution)/shard_map/reshape | solution.py:74
  63.0 6.0 %all-to-all-start = ((f32[1,8,49152]{2,0,1:T(1,128)}), f32[1,8,49152]{2,0,1:T(1,128)}, u32[]{:S(2)}, u32[]{:S(2)}) async-start(f32[1,8,49152]{2,0,1:T(1,128)} %reshape.582), calls=%async_computation | async-start | bytes 3145728 | tf_op jit(solution)/shard_map/all_to_all | solution.py:75
  69.0 37.9 %all-to-all-done = f32[1,8,49152]{2,0,1:T(1,128)} async-done(((f32[1,8,49152]{2,0,1:T(1,128)}), f32[1,8,49152]{2,0,1:T(1,128)}, u32[]{:S(2)}, u32[]{:S(2)}) %all-to-all-start) | async-done | bytes 1572896 | tf_op jit(solution)/shard_map/all_to_all | solution.py:75
  106.9 2.3 %copy.18 = f32[1,8,49152]{2,1,0:T(8,128)S(1)} copy(f32[1,8,49152]{2,0,1:T(1,128)} %all-to-all-done) | data formatting | bytes 3145728
  109.2 2.1 %gather_fusion.1 = f32[8,49152]{1,0:T(8,128)} fusion(f32[8,49152]{1,0:T(8,128)S(1)} %bitcast.62, s32[1024]{0:T(1024)S(1)} %pad_clamp_fusion), kind=kCustom, calls=%fused_computation.1 | custom fusion | bytes 3145760 | tf_op jit(solution)/shard_map/jit(_take)/gather | solution.py:76
  111.3 1.6 bitcast_select_fusion
  112.9 2.8 %copy.14 = f32[8,1,49152]{2,1,0:T(1,128)} copy(f32[8,1,49152]{2,0,1:T(8,128)S(1)} %bitcast_select_fusion) | data formatting | bytes 3145728 | tf_op jit(solution)/shard_map/jit(_take)/select_n | solution.py:76
  115.6 4.3 %all-to-all-start.1 = ((f32[8,1,49152]{2,1,0:T(1,128)}), f32[8,1,49152]{2,1,0:T(1,128)S(1)}, u32[]{:S(2)}, u32[]{:S(2)}) async-start(f32[8,1,49152]{2,1,0:T(1,128)} %copy.14), calls=%async_computation.1 | async-start | bytes 3145728 | tf_op jit(solution)/shard_map/all_to_all | solution.py:77
  120.1 1.7 gather_fusion
  121.8 0.6 fusion.55
  123.1 8.1 %psum.14 = f32[1]{0:T(128)} all-reduce(f32[1]{0:T(128)} %bitcast.13), channel_id=1, replica_groups=mesh['dom'=8,'rows'=4] {'rows'}, use_global_device_ids=true, to_apply=%region_1.2 | all-reduce | flops 1 | bytes 8 | tf_op jit(solution)/shard_map/psum | solution.py:68
  131.1 31.7 %pmax.7 = f32[]{:T(128)} all-reduce(f32[]{:T(128)} %bitcast.14), channel_id=1, replica_groups=mesh['dom'=8,'rows'=4] {'dom'}, use_global_device_ids=true, to_apply=%region_2.3 | all-reduce | flops 1 | bytes 8 | tf_op jit(solution)/shard_map/pmax | solution.py:70
  164.2 24.4 %psum.15 = f32[]{:T(128)} all-reduce(f32[]{:T(128)} %bitcast.16), channel_id=1, replica_groups=mesh['dom'=8,'rows'=4] {'dom'}, use_global_device_ids=true, to_apply=%region_3.4 | all-reduce | flops 1 | bytes 8 | tf_op jit(solution)/shard_map/psum | solution.py:71
  190.5 3.7 %reduce.2 = f32[8,49152]{1,0:T(8,128)S(1)} reduce(f32[8,1,49152]{2,1,0:T(1,128)S(1)} %all-to-all-done.1, f32[]{:T(128)} %constant.62), dimensions={1}, to_apply=%all_to_all.8.reduce_sub_computation | reduce | bytes 3145732 | tf_op jit(solution)/shard_map/all_to_all | solution.py:77
  194.2 1.6 reshape.583
  (55 shorter events, 3.4 us)
Async XLA Ops:
  2.1 5.3 %copy-start.1 = (f32[1,3,32,4096]{3,2,1,0:T(8,128)S(1)}, f32[1,3,32,4096]{3,2,1,0:T(8,128)}, u32[]{:S(2)}) copy-start(f32[1,3,32,4096]{3,2,1,0:T(8,128)} %param.6) | copy-start | bytes 4718596
  2.1 4.7 %collective-permute-start = (f32[1,1,4096]{2,1,0:T(1,128)S(1)}, f32[1,1,4096]{2,1,0:T(1,128)S(1)}, u32[]{:S(2)}, u32[]{:S(2)}) collective-permute-start(f32[1,1,4096]{2,1,0:T(1,128)S(1)} %get-tuple-element.67), channel_id=1, source_target_pairs={{1,0},{2,1},{3,2},{5,4},{6,5},{7,6},{9,8},{10,9},{11,10},{13,12},{... | collective-permute-start | bytes 49160 | tf_op jit(solution)/shard_map/ppermute | solution.py:21
  3.6 3.9 %collective-permute-start.1 = (f32[1,1,4096]{2,1,0:T(1,128)S(1)}, f32[1,1,4096]{2,1,0:T(1,128)S(1)}, u32[]{:S(2)}, u32[]{:S(2)}) collective-permute-start(f32[1,1,4096]{2,1,0:T(1,128)S(1)} %get-tuple-element.68), channel_id=1, source_target_pairs={{0,1},{1,2},{2,3},{4,5},{5,6},{6,7},{8,9},{9,10},{10,11},{12,13},{... | collective-permute-start | bytes 49160 | tf_op jit(solution)/shard_map/ppermute | solution.py:19
  7.8 6.7 %copy-start = (f32[32,4096]{1,0:T(8,128)S(1)}, f32[32,4096]{1,0:T(8,128)}, u32[]{:S(2)}) copy-start(f32[32,4096]{1,0:T(8,128)} %param.7) | copy-start | bytes 1572868
  8.0 6.9 %collective-permute-start.2 = (f32[1,1,4096]{2,1,0:T(1,128)S(1)}, f32[1,1,4096]{2,1,0:T(1,128)S(1)}, u32[]{:S(2)}, u32[]{:S(2)}) collective-permute-start(f32[1,1,4096]{2,1,0:T(1,128)S(1)} %get-tuple-element.61), channel_id=1, source_target_pairs={{1,0},{2,1},{3,2},{5,4},{6,5},{7,6},{9,8},{10,9},{11,10},{13,12},{... | collective-permute-start | bytes 49160 | tf_op jit(solution)/shard_map/ppermute | solution.py:21
  9.3 5.9 %collective-permute-start.3 = (f32[1,1,4096]{2,1,0:T(1,128)S(1)}, f32[1,1,4096]{2,1,0:T(1,128)S(1)}, u32[]{:S(2)}, u32[]{:S(2)}) collective-permute-start(f32[1,1,4096]{2,1,0:T(1,128)S(1)} %get-tuple-element.62), channel_id=1, source_target_pairs={{0,1},{1,2},{2,3},{4,5},{5,6},{6,7},{8,9},{9,10},{10,11},{12,13},{... | collective-permute-start | bytes 49160 | tf_op jit(solution)/shard_map/ppermute | solution.py:19
  15.7 6.2 %collective-permute-start.4 = (f32[1,1,4096]{2,1,0:T(1,128)S(1)}, f32[1,1,4096]{2,1,0:T(1,128)S(1)}, u32[]{:S(2)}, u32[]{:S(2)}) collective-permute-start(f32[1,1,4096]{2,1,0:T(1,128)S(1)} %get-tuple-element.59), channel_id=1, source_target_pairs={{1,0},{2,1},{3,2},{5,4},{6,5},{7,6},{9,8},{10,9},{11,10},{13,12},{... | collective-permute-start | bytes 49160 | tf_op jit(solution)/shard_map/ppermute | solution.py:21
  17.0 5.7 %collective-permute-start.5 = (f32[1,1,4096]{2,1,0:T(1,128)S(1)}, f32[1,1,4096]{2,1,0:T(1,128)S(1)}, u32[]{:S(2)}, u32[]{:S(2)}) collective-permute-start(f32[1,1,4096]{2,1,0:T(1,128)S(1)} %get-tuple-element.60), channel_id=1, source_target_pairs={{0,1},{1,2},{2,3},{4,5},{5,6},{6,7},{8,9},{9,10},{10,11},{12,13},{... | collective-permute-start | bytes 49160 | tf_op jit(solution)/shard_map/ppermute | solution.py:19
  23.2 6.6 %collective-permute-start.6 = (f32[1,1,4096]{2,1,0:T(1,128)S(1)}, f32[1,1,4096]{2,1,0:T(1,128)S(1)}, u32[]{:S(2)}, u32[]{:S(2)}) collective-permute-start(f32[1,1,4096]{2,1,0:T(1,128)S(1)} %get-tuple-element.41), channel_id=1, source_target_pairs={{1,0},{2,1},{3,2},{5,4},{6,5},{7,6},{9,8},{10,9},{11,10},{13,12},{... | collective-permute-start | bytes 49160 | tf_op jit(solution)/shard_map/ppermute | solution.py:21
  24.5 5.7 %collective-permute-start.7 = (f32[1,1,4096]{2,1,0:T(1,128)S(1)}, f32[1,1,4096]{2,1,0:T(1,128)S(1)}, u32[]{:S(2)}, u32[]{:S(2)}) collective-permute-start(f32[1,1,4096]{2,1,0:T(1,128)S(1)} %get-tuple-element.42), channel_id=1, source_target_pairs={{0,1},{1,2},{2,3},{4,5},{5,6},{6,7},{8,9},{9,10},{10,11},{12,13},{... | collective-permute-start | bytes 49160 | tf_op jit(solution)/shard_map/ppermute | solution.py:19
  30.4 6.2 %collective-permute-start.8 = (f32[1,1,4096]{2,1,0:T(1,128)S(1)}, f32[1,1,4096]{2,1,0:T(1,128)S(1)}, u32[]{:S(2)}, u32[]{:S(2)}) collective-permute-start(f32[1,1,4096]{2,1,0:T(1,128)S(1)} %get-tuple-element.39), channel_id=1, source_target_pairs={{1,0},{2,1},{3,2},{5,4},{6,5},{7,6},{9,8},{10,9},{11,10},{13,12},{... | collective-permute-start | bytes 49160 | tf_op jit(solution)/shard_map/ppermute | solution.py:21
  31.7 5.7 %collective-permute-start.9 = (f32[1,1,4096]{2,1,0:T(1,128)S(1)}, f32[1,1,4096]{2,1,0:T(1,128)S(1)}, u32[]{:S(2)}, u32[]{:S(2)}) collective-permute-start(f32[1,1,4096]{2,1,0:T(1,128)S(1)} %get-tuple-element.40), channel_id=1, source_target_pairs={{0,1},{1,2},{2,3},{4,5},{5,6},{6,7},{8,9},{9,10},{10,11},{12,13},{... | collective-permute-start | bytes 49160 | tf_op jit(solution)/shard_map/ppermute | solution.py:19
  38.0 6.6 %collective-permute-start.10 = (f32[1,1,4096]{2,1,0:T(1,128)S(1)}, f32[1,1,4096]{2,1,0:T(1,128)S(1)}, u32[]{:S(2)}, u32[]{:S(2)}) collective-permute-start(f32[1,1,4096]{2,1,0:T(1,128)S(1)} %get-tuple-element.29), channel_id=1, source_target_pairs={{1,0},{2,1},{3,2},{5,4},{6,5},{7,6},{9,8},{10,9},{11,10},{13,12},{... | collective-permute-start | bytes 49160 | tf_op jit(solution)/shard_map/ppermute | solution.py:21
  39.3 5.7 %collective-permute-start.11 = (f32[1,1,4096]{2,1,0:T(1,128)S(1)}, f32[1,1,4096]{2,1,0:T(1,128)S(1)}, u32[]{:S(2)}, u32[]{:S(2)}) collective-permute-start(f32[1,1,4096]{2,1,0:T(1,128)S(1)} %get-tuple-element.30), channel_id=1, source_target_pairs={{0,1},{1,2},{2,3},{4,5},{5,6},{6,7},{8,9},{9,10},{10,11},{12,13},{... | collective-permute-start | bytes 49160 | tf_op jit(solution)/shard_map/ppermute | solution.py:19
  45.2 6.2 %collective-permute-start.12 = (f32[1,1,4096]{2,1,0:T(1,128)S(1)}, f32[1,1,4096]{2,1,0:T(1,128)S(1)}, u32[]{:S(2)}, u32[]{:S(2)}) collective-permute-start(f32[1,1,4096]{2,1,0:T(1,128)S(1)} %get-tuple-element.27), channel_id=1, source_target_pairs={{1,0},{2,1},{3,2},{5,4},{6,5},{7,6},{9,8},{10,9},{11,10},{13,12},{... | collective-permute-start | bytes 49160 | tf_op jit(solution)/shard_map/ppermute | solution.py:21
  46.5 5.7 %collective-permute-start.13 = (f32[1,1,4096]{2,1,0:T(1,128)S(1)}, f32[1,1,4096]{2,1,0:T(1,128)S(1)}, u32[]{:S(2)}, u32[]{:S(2)}) collective-permute-start(f32[1,1,4096]{2,1,0:T(1,128)S(1)} %get-tuple-element.28), channel_id=1, source_target_pairs={{0,1},{1,2},{2,3},{4,5},{5,6},{6,7},{8,9},{9,10},{10,11},{12,13},{... | collective-permute-start | bytes 49160 | tf_op jit(solution)/shard_map/ppermute | solution.py:19
  52.7 6.2 %collective-permute-start.14 = (f32[1,1,4096]{2,1,0:T(1,128)S(1)}, f32[1,1,4096]{2,1,0:T(1,128)S(1)}, u32[]{:S(2)}, u32[]{:S(2)}) collective-permute-start(f32[1,1,4096]{2,1,0:T(1,128)S(1)} %get-tuple-element.21), channel_id=1, source_target_pairs={{1,0},{2,1},{3,2},{5,4},{6,5},{7,6},{9,8},{10,9},{11,10},{13,12},{... | collective-permute-start | bytes 49160 | tf_op jit(solution)/shard_map/ppermute | solution.py:21
  54.0 5.7 %collective-permute-start.15 = (f32[1,1,4096]{2,1,0:T(1,128)S(1)}, f32[1,1,4096]{2,1,0:T(1,128)S(1)}, u32[]{:S(2)}, u32[]{:S(2)}) collective-permute-start(f32[1,1,4096]{2,1,0:T(1,128)S(1)} %get-tuple-element.22), channel_id=1, source_target_pairs={{0,1},{1,2},{2,3},{4,5},{5,6},{6,7},{8,9},{9,10},{10,11},{12,13},{... | collective-permute-start | bytes 49160 | tf_op jit(solution)/shard_map/ppermute | solution.py:19
  63.0 6.0 %copy-start.5 = (s32[8]{0:T(128)S(1)}, s32[8]{0:T(128)}, u32[]{:S(2)}) copy-start(s32[8]{0:T(128)} %param.11) | copy-start | bytes 100
  63.0 43.9 %all-to-all-start = ((f32[1,8,49152]{2,0,1:T(1,128)}), f32[1,8,49152]{2,0,1:T(1,128)}, u32[]{:S(2)}, u32[]{:S(2)}) async-start(f32[1,8,49152]{2,0,1:T(1,128)} %reshape.582), calls=%async_computation | async-start | bytes 3145728 | tf_op jit(solution)/shard_map/all_to_all | solution.py:75
  115.6 4.3 %copy-start.2 = (s32[256]{0:T(256)S(1)}, s32[256]{0:T(256)}, u32[]{:S(2)}) copy-start(s32[256]{0:T(256)} %param.8) | copy-start | bytes 3076
  115.6 74.8 %all-to-all-start.1 = ((f32[8,1,49152]{2,1,0:T(1,128)}), f32[8,1,49152]{2,1,0:T(1,128)S(1)}, u32[]{:S(2)}, u32[]{:S(2)}) async-start(f32[8,1,49152]{2,1,0:T(1,128)} %copy.14), calls=%async_computation.1 | async-start | bytes 3145728 | tf_op jit(solution)/shard_map/all_to_all | solution.py:77
  119.9 1.9 copy-start.3
  119.9 1.9 copy-start.4
where the time goes:
time: 198 us; the launch traced here: 197 us
  blocking collectives  64.2 us (32%)
  starting transfers between devices  58 us (29%)
  waiting for transfers between devices  42.5 us (21%)
  local copies, waits for them, and re-layouts  15.8 us (8%)
  other arithmetic  10.4 us (5%)
  between operations  5.97 us (3%)
    all_to_all x1, waiting for transfers between devices, shards(): lax.all_to_all(subregion_tiles, 'dom', split_axis=1, concat_axis=0, tiled...  37.9 us
    ppermute x8, starting transfers between devices, extended(): lax.ppermute(tail, axis, [(i, (i + 1) % count) for i in range(ends)])  37.3 us
    pmax x1, blocking collectives, shards(): peak = lax.pmax(local_peak, 'dom')  31.7 us
    psum x1, blocking collectives, shards(): total = lax.psum(jnp.sum(jnp.exp(loglik - peak)), 'dom')  24.4 us
    ppermute x8, starting transfers between devices, extended(): lax.ppermute(head, axis, [((i + 1) % count, i) for i in range(ends)])  10.5 us
    psum x1, blocking collectives, shards(): loglik = lax.psum(-0.5 * jnp.sum(misfit, axis=1), 'rows')  8.06 us
    all_to_all x1, starting transfers between devices, shards(): lax.all_to_all(subregion_tiles, 'dom', split_axis=1, concat_axis=0, tiled...  5.97 us
    ppermute x8, waiting for transfers between devices, extended(): lax.ppermute(tail, axis, [(i, (i + 1) % count) for i in range(ends)])  4.65 us
  transfers between devices with their start and end apart: 18, of which 9 were waited for; matrix products, arithmetic and copies ran while one was open for 2% of the time, Pallas kernels for 0%

commit v1 on v0

--- a/solution.py
+++ b/solution.py
@@ -65,7 +65,7 @@
     inside = (offset >= 0) & (offset < slab_cells)
     values = jnp.take(flat, jnp.clip(offset, 0, slab_cells - 1), axis=1)
     misfit = jnp.where(inside[None, :], (obs_value[None, :] - values) ** 2 / obs_var[None, :], 0.0)
-    loglik = lax.psum(-0.5 * jnp.sum(misfit, axis=1), "rows")
+    loglik = jnp.sum(lax.all_gather(-0.5 * jnp.sum(misfit, axis=1), "rows"), axis=0)
     local_peak = jnp.max(loglik)
     peak = lax.pmax(local_peak, "dom")
     total = lax.psum(jnp.sum(jnp.exp(loglik - peak)), "dom")

time: 198 us -> 197 us (level)
  blocking collectives: 64.2 us -> 61.6 us
    psum x1 -> x0, blocking collectives: 8.06 us -> none  [shards(): loglik = lax.psum(-0.5 * jnp.sum(misfit, axis=1), 'rows')]
    unnamed x0 -> x1, blocking collectives: none -> 7.08 us
  transfers between devices with their start and end apart: 18 -> 18, of which waited for: 9 -> 9; matrix products, arithmetic and copies ran while one was open for 2% -> 3% of each run, Pallas kernels for 0% -> 0%
where the time goes in v1:
time: 197 us; the launch traced here: 196 us
  blocking collectives  61.6 us (31%)
  starting transfers between devices  58 us (29%)
  waiting for transfers between devices  42.5 us (22%)
  local copies, waits for them, and re-layouts  17.2 us (9%)
  other arithmetic  11 us (6%)
  between operations  6.08 us (3%)
    all_to_all x1, waiting for transfers between devices, shards(): lax.all_to_all(subregion_tiles, 'dom', split_axis=1, concat_axis=0, tiled...  37.9 us
    ppermute x8, starting transfers between devices, extended(): lax.ppermute(tail, axis, [(i, (i + 1) % count) for i in range(ends)])  37.3 us
    pmax x1, blocking collectives, shards(): peak = lax.pmax(local_peak, 'dom')  30.8 us
    psum x1, blocking collectives, shards(): total = lax.psum(jnp.sum(jnp.exp(loglik - peak)), 'dom')  23.8 us
    ppermute x8, starting transfers between devices, extended(): lax.ppermute(head, axis, [((i + 1) % count, i) for i in range(ends)])  10.5 us
    unnamed x1, blocking collectives  7.08 us
    all_to_all x1, starting transfers between devices, shards(): lax.all_to_all(subregion_tiles, 'dom', split_axis=1, concat_axis=0, tiled...  5.97 us
    ppermute x8, waiting for transfers between devices, extended(): lax.ppermute(tail, axis, [(i, (i + 1) % count) for i in range(ends)])  4.65 us
  transfers between devices with their start and end apart: 18, of which 9 were waited for; matrix products, arithmetic and copies ran while one was open for 3% of the time, Pallas kernels for 0%

profile of v1, /device:TPU:0, one launch (start us, length us, event | category | flops | bytes accessed | tf_op | source)
XLA Modules:
  0.0 196.4 jit_solution(10204052808866241028)
XLA Ops:
  0.6 1.5 fusion.51
  2.1 1.4 collective-permute-start
  3.6 3.0 %collective-permute-start.1 = (f32[1,1,4096]{2,1,0:T(1,128)S(1)}, f32[1,1,4096]{2,1,0:T(1,128)S(1)}, u32[]{:S(2)}, u32[]{:S(2)}) collective-permute-start(f32[1,1,4096]{2,1,0:T(1,128)S(1)} %get-tuple-element.68), channel_id=1, source_target_pairs={{0,1},{1,2},{2,3},{4,5},{5,6},{6,7},{8,9},{9,10},{10,11},{12,13},{... | collective-permute-start | bytes 49160 | tf_op jit(solution)/shard_map/ppermute | solution.py:19
  6.9 0.5 collective-permute-done.1
  7.4 0.2 fusion.32
  8.0 1.3 collective-permute-start.2
  9.3 5.1 %collective-permute-start.3 = (f32[1,1,4096]{2,1,0:T(1,128)S(1)}, f32[1,1,4096]{2,1,0:T(1,128)S(1)}, u32[]{:S(2)}, u32[]{:S(2)}) collective-permute-start(f32[1,1,4096]{2,1,0:T(1,128)S(1)} %get-tuple-element.62), channel_id=1, source_target_pairs={{0,1},{1,2},{2,3},{4,5},{5,6},{6,7},{8,9},{9,10},{10,11},{12,13},{... | collective-permute-start | bytes 49160 | tf_op jit(solution)/shard_map/ppermute | solution.py:19
  14.9 0.4 collective-permute-done.3
  15.3 0.3 bitcast_multiply_fusion.5
  15.7 1.3 collective-permute-start.4
  17.0 4.9 %collective-permute-start.5 = (f32[1,1,4096]{2,1,0:T(1,128)S(1)}, f32[1,1,4096]{2,1,0:T(1,128)S(1)}, u32[]{:S(2)}, u32[]{:S(2)}) collective-permute-start(f32[1,1,4096]{2,1,0:T(1,128)S(1)} %get-tuple-element.60), channel_id=1, source_target_pairs={{0,1},{1,2},{2,3},{4,5},{5,6},{6,7},{8,9},{9,10},{10,11},{12,13},{... | collective-permute-start | bytes 49160 | tf_op jit(solution)/shard_map/ppermute | solution.py:19
  21.9 0.7 collective-permute-done.5
  23.2 1.3 collective-permute-start.6
  24.5 4.9 %collective-permute-start.7 = (f32[1,1,4096]{2,1,0:T(1,128)S(1)}, f32[1,1,4096]{2,1,0:T(1,128)S(1)}, u32[]{:S(2)}, u32[]{:S(2)}) collective-permute-start(f32[1,1,4096]{2,1,0:T(1,128)S(1)} %get-tuple-element.42), channel_id=1, source_target_pairs={{0,1},{1,2},{2,3},{4,5},{5,6},{6,7},{8,9},{9,10},{10,11},{12,13},{... | collective-permute-start | bytes 49160 | tf_op jit(solution)/shard_map/ppermute | solution.py:19
  29.8 0.4 collective-permute-done.7
  30.4 1.3 collective-permute-start.8
  31.7 4.9 %collective-permute-start.9 = (f32[1,1,4096]{2,1,0:T(1,128)S(1)}, f32[1,1,4096]{2,1,0:T(1,128)S(1)}, u32[]{:S(2)}, u32[]{:S(2)}) collective-permute-start(f32[1,1,4096]{2,1,0:T(1,128)S(1)} %get-tuple-element.40), channel_id=1, source_target_pairs={{0,1},{1,2},{2,3},{4,5},{5,6},{6,7},{8,9},{9,10},{10,11},{12,13},{... | collective-permute-start | bytes 49160 | tf_op jit(solution)/shard_map/ppermute | solution.py:19
  36.7 0.7 collective-permute-done.9
  37.4 0.3 fusion.16
  38.0 1.3 collective-permute-start.10
  39.3 4.9 %collective-permute-start.11 = (f32[1,1,4096]{2,1,0:T(1,128)S(1)}, f32[1,1,4096]{2,1,0:T(1,128)S(1)}, u32[]{:S(2)}, u32[]{:S(2)}) collective-permute-start(f32[1,1,4096]{2,1,0:T(1,128)S(1)} %get-tuple-element.30), channel_id=1, source_target_pairs={{0,1},{1,2},{2,3},{4,5},{5,6},{6,7},{8,9},{9,10},{10,11},{12,13},{... | collective-permute-start | bytes 49160 | tf_op jit(solution)/shard_map/ppermute | solution.py:19
  44.6 0.4 collective-permute-done.11
  45.2 1.3 collective-permute-start.12
  46.5 4.9 %collective-permute-start.13 = (f32[1,1,4096]{2,1,0:T(1,128)S(1)}, f32[1,1,4096]{2,1,0:T(1,128)S(1)}, u32[]{:S(2)}, u32[]{:S(2)}) collective-permute-start(f32[1,1,4096]{2,1,0:T(1,128)S(1)} %get-tuple-element.28), channel_id=1, source_target_pairs={{0,1},{1,2},{2,3},{4,5},{5,6},{6,7},{8,9},{9,10},{10,11},{12,13},{... | collective-permute-start | bytes 49160 | tf_op jit(solution)/shard_map/ppermute | solution.py:19
  51.5 0.7 collective-permute-done.13
  52.2 0.3 fusion.8
  52.7 1.3 collective-permute-start.14
  54.0 4.9 %collective-permute-start.15 = (f32[1,1,4096]{2,1,0:T(1,128)S(1)}, f32[1,1,4096]{2,1,0:T(1,128)S(1)}, u32[]{:S(2)}, u32[]{:S(2)}) collective-permute-start(f32[1,1,4096]{2,1,0:T(1,128)S(1)} %get-tuple-element.22), channel_id=1, source_target_pairs={{0,1},{1,2},{2,3},{4,5},{5,6},{6,7},{8,9},{9,10},{10,11},{12,13},{... | collective-permute-start | bytes 49160 | tf_op jit(solution)/shard_map/ppermute | solution.py:19
  59.0 0.7 collective-permute-done.15
  59.7 0.3 fusion.4
  60.2 2.8 %reshape.589 = f32[1,8,49152]{2,0,1:T(1,128)} reshape(f32[1,3,32,4096]{3,2,1,0:T(8,128)S(1)} %pad_maximum_fusion) | data formatting | bytes 3145728 | tf_op jit(solution)/shard_map/reshape | solution.py:74
  63.0 6.0 %all-to-all-start = ((f32[1,8,49152]{2,0,1:T(1,128)}), f32[1,8,49152]{2,0,1:T(1,128)}, u32[]{:S(2)}, u32[]{:S(2)}) async-start(f32[1,8,49152]{2,0,1:T(1,128)} %reshape.589), calls=%async_computation | async-start | bytes 3145728 | tf_op jit(solution)/shard_map/all_to_all | solution.py:75
  69.0 37.9 %all-to-all-done = f32[1,8,49152]{2,0,1:T(1,128)} async-done(((f32[1,8,49152]{2,0,1:T(1,128)}), f32[1,8,49152]{2,0,1:T(1,128)}, u32[]{:S(2)}, u32[]{:S(2)}) %all-to-all-start) | async-done | bytes 1572896 | tf_op jit(solution)/shard_map/all_to_all | solution.py:75
  106.9 2.3 %copy.18 = f32[1,8,49152]{2,1,0:T(8,128)S(1)} copy(f32[1,8,49152]{2,0,1:T(1,128)} %all-to-all-done) | data formatting | bytes 3145728
  109.2 2.1 %gather_fusion.1 = f32[8,49152]{1,0:T(8,128)} fusion(f32[8,49152]{1,0:T(8,128)S(1)} %bitcast.60, s32[1024]{0:T(1024)S(1)} %pad_clamp_fusion), kind=kCustom, calls=%fused_computation.1 | custom fusion | bytes 3145760 | tf_op jit(solution)/shard_map/jit(_take)/gather | solution.py:76
  111.3 1.6 bitcast_select_fusion
  112.9 2.8 %copy.14 = f32[8,1,49152]{2,1,0:T(1,128)} copy(f32[8,1,49152]{2,0,1:T(8,128)S(1)} %bitcast_select_fusion) | data formatting | bytes 3145728 | tf_op jit(solution)/shard_map/jit(_take)/select_n | solution.py:76
  115.6 4.3 %all-to-all-start.1 = ((f32[8,1,49152]{2,1,0:T(1,128)}), f32[8,1,49152]{2,1,0:T(1,128)S(1)}, u32[]{:S(2)}, u32[]{:S(2)}) async-start(f32[8,1,49152]{2,1,0:T(1,128)} %copy.14), calls=%async_computation.1 | async-start | bytes 3145728 | tf_op jit(solution)/shard_map/all_to_all | solution.py:77
  119.9 0.6 dynamic-slice
  120.7 1.7 gather_fusion
  122.5 0.6 fusion.55
  123.7 0.7 dynamic-update-slice
  124.5 7.1 %all-reduce = f32[4]{0:T(128)S(1)} all-reduce(f32[4]{0:T(128)S(1)} %dynamic-update-slice), channel_id=1, replica_groups=mesh['dom'=8,'rows'=4] {'rows'}, use_global_device_ids=true, to_apply=%add | all-reduce | flops 4 | bytes 32
  131.5 0.6 reduce.3
  132.1 30.8 %pmax.7 = f32[]{:T(128)} all-reduce(f32[]{:T(128)} %reduce.3), channel_id=1, replica_groups=mesh['dom'=8,'rows'=4] {'dom'}, use_global_device_ids=true, to_apply=%region_2.3 | all-reduce | flops 1 | bytes 8 | tf_op jit(solution)/shard_map/pmax | solution.py:70
  164.2 23.8 %psum.7 = f32[]{:T(128)} all-reduce(f32[]{:T(128)S(6)} %exp.4), channel_id=1, replica_groups=mesh['dom'=8,'rows'=4] {'dom'}, use_global_device_ids=true, to_apply=%region_3.4 | all-reduce | flops 1 | bytes 8 | tf_op jit(solution)/shard_map/psum | solution.py:71
  190.0 3.7 %reduce.5 = f32[8,49152]{1,0:T(8,128)S(1)} reduce(f32[8,1,49152]{2,1,0:T(1,128)S(1)} %all-to-all-done.1, f32[]{:T(128)} %constant.68), dimensions={1}, to_apply=%all_to_all.8.reduce_sub_computation | reduce | bytes 3145732 | tf_op jit(solution)/shard_map/all_to_all | solution.py:77
  193.7 1.6 reshape.590
  (61 shorter events, 4.1 us)
Async XLA Ops:
  2.1 5.3 %copy-start.1 = (f32[1,3,32,4096]{3,2,1,0:T(8,128)S(1)}, f32[1,3,32,4096]{3,2,1,0:T(8,128)}, u32[]{:S(2)}) copy-start(f32[1,3,32,4096]{3,2,1,0:T(8,128)} %param.6) | copy-start | bytes 4718596
  2.1 4.7 %collective-permute-start = (f32[1,1,4096]{2,1,0:T(1,128)S(1)}, f32[1,1,4096]{2,1,0:T(1,128)S(1)}, u32[]{:S(2)}, u32[]{:S(2)}) collective-permute-start(f32[1,1,4096]{2,1,0:T(1,128)S(1)} %get-tuple-element.67), channel_id=1, source_target_pairs={{1,0},{2,1},{3,2},{5,4},{6,5},{7,6},{9,8},{10,9},{11,10},{13,12},{... | collective-permute-start | bytes 49160 | tf_op jit(solution)/shard_map/ppermute | solution.py:21
  3.6 3.9 %collective-permute-start.1 = (f32[1,1,4096]{2,1,0:T(1,128)S(1)}, f32[1,1,4096]{2,1,0:T(1,128)S(1)}, u32[]{:S(2)}, u32[]{:S(2)}) collective-permute-start(f32[1,1,4096]{2,1,0:T(1,128)S(1)} %get-tuple-element.68), channel_id=1, source_target_pairs={{0,1},{1,2},{2,3},{4,5},{5,6},{6,7},{8,9},{9,10},{10,11},{12,13},{... | collective-permute-start | bytes 49160 | tf_op jit(solution)/shard_map/ppermute | solution.py:19
  7.8 6.7 %copy-start = (f32[32,4096]{1,0:T(8,128)S(1)}, f32[32,4096]{1,0:T(8,128)}, u32[]{:S(2)}) copy-start(f32[32,4096]{1,0:T(8,128)} %param.7) | copy-start | bytes 1572868
  8.0 6.9 %collective-permute-start.2 = (f32[1,1,4096]{2,1,0:T(1,128)S(1)}, f32[1,1,4096]{2,1,0:T(1,128)S(1)}, u32[]{:S(2)}, u32[]{:S(2)}) collective-permute-start(f32[1,1,4096]{2,1,0:T(1,128)S(1)} %get-tuple-element.61), channel_id=1, source_target_pairs={{1,0},{2,1},{3,2},{5,4},{6,5},{7,6},{9,8},{10,9},{11,10},{13,12},{... | collective-permute-start | bytes 49160 | tf_op jit(solution)/shard_map/ppermute | solution.py:21
  9.3 5.9 %collective-permute-start.3 = (f32[1,1,4096]{2,1,0:T(1,128)S(1)}, f32[1,1,4096]{2,1,0:T(1,128)S(1)}, u32[]{:S(2)}, u32[]{:S(2)}) collective-permute-start(f32[1,1,4096]{2,1,0:T(1,128)S(1)} %get-tuple-element.62), channel_id=1, source_target_pairs={{0,1},{1,2},{2,3},{4,5},{5,6},{6,7},{8,9},{9,10},{10,11},{12,13},{... | collective-permute-start | bytes 49160 | tf_op jit(solution)/shard_map/ppermute | solution.py:19
  15.7 6.2 %collective-permute-start.4 = (f32[1,1,4096]{2,1,0:T(1,128)S(1)}, f32[1,1,4096]{2,1,0:T(1,128)S(1)}, u32[]{:S(2)}, u32[]{:S(2)}) collective-permute-start(f32[1,1,4096]{2,1,0:T(1,128)S(1)} %get-tuple-element.59), channel_id=1, source_target_pairs={{1,0},{2,1},{3,2},{5,4},{6,5},{7,6},{9,8},{10,9},{11,10},{13,12},{... | collective-permute-start | bytes 49160 | tf_op jit(solution)/shard_map/ppermute | solution.py:21
  17.0 5.7 %collective-permute-start.5 = (f32[1,1,4096]{2,1,0:T(1,128)S(1)}, f32[1,1,4096]{2,1,0:T(1,128)S(1)}, u32[]{:S(2)}, u32[]{:S(2)}) collective-permute-start(f32[1,1,4096]{2,1,0:T(1,128)S(1)} %get-tuple-element.60), channel_id=1, source_target_pairs={{0,1},{1,2},{2,3},{4,5},{5,6},{6,7},{8,9},{9,10},{10,11},{12,13},{... | collective-permute-start | bytes 49160 | tf_op jit(solution)/shard_map/ppermute | solution.py:19
  23.2 6.6 %collective-permute-start.6 = (f32[1,1,4096]{2,1,0:T(1,128)S(1)}, f32[1,1,4096]{2,1,0:T(1,128)S(1)}, u32[]{:S(2)}, u32[]{:S(2)}) collective-permute-start(f32[1,1,4096]{2,1,0:T(1,128)S(1)} %get-tuple-element.41), channel_id=1, source_target_pairs={{1,0},{2,1},{3,2},{5,4},{6,5},{7,6},{9,8},{10,9},{11,10},{13,12},{... | collective-permute-start | bytes 49160 | tf_op jit(solution)/shard_map/ppermute | solution.py:21
  24.5 5.7 %collective-permute-start.7 = (f32[1,1,4096]{2,1,0:T(1,128)S(1)}, f32[1,1,4096]{2,1,0:T(1,128)S(1)}, u32[]{:S(2)}, u32[]{:S(2)}) collective-permute-start(f32[1,1,4096]{2,1,0:T(1,128)S(1)} %get-tuple-element.42), channel_id=1, source_target_pairs={{0,1},{1,2},{2,3},{4,5},{5,6},{6,7},{8,9},{9,10},{10,11},{12,13},{... | collective-permute-start | bytes 49160 | tf_op jit(solution)/shard_map/ppermute | solution.py:19
  30.4 6.2 %collective-permute-start.8 = (f32[1,1,4096]{2,1,0:T(1,128)S(1)}, f32[1,1,4096]{2,1,0:T(1,128)S(1)}, u32[]{:S(2)}, u32[]{:S(2)}) collective-permute-start(f32[1,1,4096]{2,1,0:T(1,128)S(1)} %get-tuple-element.39), channel_id=1, source_target_pairs={{1,0},{2,1},{3,2},{5,4},{6,5},{7,6},{9,8},{10,9},{11,10},{13,12},{... | collective-permute-start | bytes 49160 | tf_op jit(solution)/shard_map/ppermute | solution.py:21
  31.7 5.7 %collective-permute-start.9 = (f32[1,1,4096]{2,1,0:T(1,128)S(1)}, f32[1,1,4096]{2,1,0:T(1,128)S(1)}, u32[]{:S(2)}, u32[]{:S(2)}) collective-permute-start(f32[1,1,4096]{2,1,0:T(1,128)S(1)} %get-tuple-element.40), channel_id=1, source_target_pairs={{0,1},{1,2},{2,3},{4,5},{5,6},{6,7},{8,9},{9,10},{10,11},{12,13},{... | collective-permute-start | bytes 49160 | tf_op jit(solution)/shard_map/ppermute | solution.py:19
  38.0 6.6 %collective-permute-start.10 = (f32[1,1,4096]{2,1,0:T(1,128)S(1)}, f32[1,1,4096]{2,1,0:T(1,128)S(1)}, u32[]{:S(2)}, u32[]{:S(2)}) collective-permute-start(f32[1,1,4096]{2,1,0:T(1,128)S(1)} %get-tuple-element.29), channel_id=1, source_target_pairs={{1,0},{2,1},{3,2},{5,4},{6,5},{7,6},{9,8},{10,9},{11,10},{13,12},{... | collective-permute-start | bytes 49160 | tf_op jit(solution)/shard_map/ppermute | solution.py:21
  39.3 5.7 %collective-permute-start.11 = (f32[1,1,4096]{2,1,0:T(1,128)S(1)}, f32[1,1,4096]{2,1,0:T(1,128)S(1)}, u32[]{:S(2)}, u32[]{:S(2)}) collective-permute-start(f32[1,1,4096]{2,1,0:T(1,128)S(1)} %get-tuple-element.30), channel_id=1, source_target_pairs={{0,1},{1,2},{2,3},{4,5},{5,6},{6,7},{8,9},{9,10},{10,11},{12,13},{... | collective-permute-start | bytes 49160 | tf_op jit(solution)/shard_map/ppermute | solution.py:19
  45.2 6.2 %collective-permute-start.12 = (f32[1,1,4096]{2,1,0:T(1,128)S(1)}, f32[1,1,4096]{2,1,0:T(1,128)S(1)}, u32[]{:S(2)}, u32[]{:S(2)}) collective-permute-start(f32[1,1,4096]{2,1,0:T(1,128)S(1)} %get-tuple-element.27), channel_id=1, source_target_pairs={{1,0},{2,1},{3,2},{5,4},{6,5},{7,6},{9,8},{10,9},{11,10},{13,12},{... | collective-permute-start | bytes 49160 | tf_op jit(solution)/shard_map/ppermute | solution.py:21
  46.5 5.7 %collective-permute-start.13 = (f32[1,1,4096]{2,1,0:T(1,128)S(1)}, f32[1,1,4096]{2,1,0:T(1,128)S(1)}, u32[]{:S(2)}, u32[]{:S(2)}) collective-permute-start(f32[1,1,4096]{2,1,0:T(1,128)S(1)} %get-tuple-element.28), channel_id=1, source_target_pairs={{0,1},{1,2},{2,3},{4,5},{5,6},{6,7},{8,9},{9,10},{10,11},{12,13},{... | collective-permute-start | bytes 49160 | tf_op jit(solution)/shard_map/ppermute | solution.py:19
  52.7 6.2 %collective-permute-start.14 = (f32[1,1,4096]{2,1,0:T(1,128)S(1)}, f32[1,1,4096]{2,1,0:T(1,128)S(1)}, u32[]{:S(2)}, u32[]{:S(2)}) collective-permute-start(f32[1,1,4096]{2,1,0:T(1,128)S(1)} %get-tuple-element.21), channel_id=1, source_target_pairs={{1,0},{2,1},{3,2},{5,4},{6,5},{7,6},{9,8},{10,9},{11,10},{13,12},{... | collective-permute-start | bytes 49160 | tf_op jit(solution)/shard_map/ppermute | solution.py:21
  54.0 5.7 %collective-permute-start.15 = (f32[1,1,4096]{2,1,0:T(1,128)S(1)}, f32[1,1,4096]{2,1,0:T(1,128)S(1)}, u32[]{:S(2)}, u32[]{:S(2)}) collective-permute-start(f32[1,1,4096]{2,1,0:T(1,128)S(1)} %get-tuple-element.22), channel_id=1, source_target_pairs={{0,1},{1,2},{2,3},{4,5},{5,6},{6,7},{8,9},{9,10},{10,11},{12,13},{... | collective-permute-start | bytes 49160 | tf_op jit(solution)/shard_map/ppermute | solution.py:19
  63.0 6.0 %copy-start.5 = (s32[8]{0:T(128)S(1)}, s32[8]{0:T(128)}, u32[]{:S(2)}) copy-start(s32[8]{0:T(128)} %param.11) | copy-start | bytes 100
  63.0 43.9 %all-to-all-start = ((f32[1,8,49152]{2,0,1:T(1,128)}), f32[1,8,49152]{2,0,1:T(1,128)}, u32[]{:S(2)}, u32[]{:S(2)}) async-start(f32[1,8,49152]{2,0,1:T(1,128)} %reshape.589), calls=%async_computation | async-start | bytes 3145728 | tf_op jit(solution)/shard_map/all_to_all | solution.py:75
  115.6 4.3 %copy-start.6 = (u32[32]{0:T(128)S(1)}, u32[32]{0:T(128)}, u32[]{:S(2)}) copy-start(u32[32]{0:T(128)} %constant.64) | copy-start | bytes 388
  115.6 5.0 %copy-start.2 = (s32[256]{0:T(256)S(1)}, s32[256]{0:T(256)}, u32[]{:S(2)}) copy-start(s32[256]{0:T(256)} %param.8) | copy-start | bytes 3076
  115.6 74.3 %all-to-all-start.1 = ((f32[8,1,49152]{2,1,0:T(1,128)}), f32[8,1,49152]{2,1,0:T(1,128)S(1)}, u32[]{:S(2)}, u32[]{:S(2)}) async-start(f32[8,1,49152]{2,1,0:T(1,128)} %copy.14), calls=%async_computation.1 | async-start | bytes 3145728 | tf_op jit(solution)/shard_map/all_to_all | solution.py:77
  119.9 2.5 %copy-start.3 = (f32[256]{0:T(256)S(1)}, f32[256]{0:T(256)}, u32[]{:S(2)}) copy-start(f32[256]{0:T(256)} %param.10) | copy-start | bytes 3076
  119.9 2.5 %copy-start.4 = (f32[256]{0:T(256)S(1)}, f32[256]{0:T(256)}, u32[]{:S(2)}) copy-start(f32[256]{0:T(256)} %param.9) | copy-start | bytes 3076
